TPU v7x, 32 devices: a whole 2x2x4 slice. The times are simulated.
32 devices in a mesh: dp: 4 (over y, x), psg: 8 (over z, core).
Axes of the slice: x: 2, y: 2, z: 4, core: 2. Of those that a mesh axis runs over, the one named last changes fastest.
Arguments:
- queries: bfloat16 [4, 128, 2048], P('dp', None, 'psg'), may hold values from -4 to 4
- keys: bfloat16 [4, 16, 256, 2048], P('dp', 'psg'), may hold values from -4 to 4
- values: bfloat16 [4, 16, 256, 2048], P('dp', 'psg'), may hold values from -6 to 6
- lengths: int32 [4, 16], P('dp', 'psg'), may hold values from 16 to 256, as said below
- out_weight: bfloat16 [4096, 2048], P('psg'), may hold values from -0.125 to 0.125
- out_cotangent: bfloat16 [4, 128, 4096], P('dp', None, 'psg'), may hold values from -6 to 6
Outputs:
- layer_out: bfloat16 [4, 128, 4096], P('dp', None, 'psg')
- weight_grad: float32 [4096, 2048], P('psg')
- query_grad: bfloat16 [4, 128, 2048], P('dp', None, 'psg')
- key_grad: bfloat16 [4, 16, 256, 2048], P('dp', 'psg')
- value_grad: bfloat16 [4, 16, 256, 2048], P('dp', 'psg')
Inputs may be any that keep to these rules, and one draw needn't show every extreme that they name: `lengths`: every passage has at least 16 valid tokens, counted from its start; in every question some passage has all 256.
All inputs are finite; a program needn't handle non-finite values.
Results may differ from a plain program's by a relative error of at most 0.025.
Values may be sent and summed in bfloat16 or wider, within the bound.
No kernel may reach another device: no remote copies, remote signals or barrier semaphores. Data moves between devices by JAX's collectives and lax.ppermute only.
A program may use at most 64 MiB of HBM per device.

v0:
```python
import jax
import jax.numpy as jnp
from jax import lax
from jax.sharding import PartitionSpec as P

HEAD_COUNT = 32
HEAD_SIZE = 64


def spread_heads(factor):
    return jnp.transpose(factor, (0, 2, 1))[..., None]


def local_weights(scores, valid_keys, row_max):
    return jnp.where(valid_keys, jnp.exp(scores - row_max[..., None]), 0.0)


def weighted_values(weights, value_heads):
    output = jnp.einsum(
        "bhik,bkhe->bihe",
        weights.astype(jnp.bfloat16),
        value_heads,
        preferred_element_type=jnp.float32,
    )
    return output.reshape(output.shape[0], output.shape[1], -1)


def per_device(queries, keys, values, lengths, out_weight, out_cotangent):
    question_count = keys.shape[0]
    key_count = keys.shape[1] * keys.shape[2]
    inner_dim = keys.shape[3]
    answer_len = queries.shape[1]
    head_split = (question_count, answer_len, HEAD_COUNT, HEAD_SIZE)
    query_full = lax.all_gather(queries, "psg", axis=2, tiled=True)
    query_heads = query_full.reshape(head_split)
    key_heads = keys.reshape(question_count, key_count, HEAD_COUNT, HEAD_SIZE)
    value_heads = values.reshape(question_count, key_count, HEAD_COUNT, HEAD_SIZE)
    positions = jnp.arange(keys.shape[2], dtype=jnp.int32)
    valid_keys = (positions[None, None, :] < lengths[:, :, None]).reshape(
        question_count, 1, 1, key_count
    )
    scores = jnp.einsum(
        "bihe,bkhe->bhik", query_heads, key_heads, preferred_element_type=jnp.float32
    )
    local_max = jnp.max(jnp.where(valid_keys, scores, -jnp.inf), axis=3)
    row_max = lax.pmax(local_max, "psg")
    weights = local_weights(scores, valid_keys, row_max)
    row_sum, output = lax.psum(
        (jnp.sum(weights, axis=3), weighted_values(weights, value_heads)), "psg"
    )
    context = (
        (output.reshape(head_split) / spread_heads(row_sum))
        .astype(jnp.bfloat16)
        .reshape(question_count, answer_len, inner_dim)
    )
    context_rows = context.reshape(question_count * answer_len, inner_dim)
    grad_rows = out_cotangent.reshape(question_count * answer_len, -1)
    layer_out = jnp.dot(context_rows, out_weight.T, preferred_element_type=jnp.float32).astype(
        jnp.bfloat16
    )
    layer_out = layer_out.reshape(question_count, answer_len, -1)
    weight_grad = lax.psum(
        jnp.dot(grad_rows.T, context_rows, preferred_element_type=jnp.float32).astype(jnp.bfloat16),
        "dp",
    ).astype(jnp.float32)
    context_grad = lax.psum(
        jnp.dot(grad_rows, out_weight, preferred_element_type=jnp.float32), "psg"
    ).astype(jnp.bfloat16)
    grad_heads = context_grad.reshape(head_split)
    products = context_grad.reshape(question_count, answer_len, inner_dim).astype(
        jnp.float32
    ) * context.astype(jnp.float32)
    row_dots = jnp.transpose(jnp.sum(products.reshape(head_split), axis=3), (0, 2, 1))
    probs = weights / row_sum[..., None]
    prob_grad = jnp.einsum(
        "bihe,bkhe->bhik", grad_heads, value_heads, preferred_element_type=jnp.float32
    )
    score_grad = (probs * (prob_grad - row_dots[..., None])).astype(jnp.bfloat16)
    value_grad = jnp.einsum(
        "bhik,bihe->bkhe",
        probs.astype(jnp.bfloat16),
        grad_heads,
        preferred_element_type=jnp.float32,
    )
    value_grad = value_grad.astype(jnp.bfloat16).reshape(values.shape)
    key_grad = jnp.einsum(
        "bhik,bihe->bkhe", score_grad, query_heads, preferred_element_type=jnp.float32
    )
    key_grad = key_grad.astype(jnp.bfloat16).reshape(keys.shape)
    query_terms = jnp.einsum(
        "bhik,bkhe->bihe", score_grad, key_heads, preferred_element_type=jnp.float32
    )
    query_terms = query_terms.reshape(question_count, answer_len, inner_dim)
    query_grad = lax.psum_scatter(query_terms, "psg", scatter_dimension=2, tiled=True).astype(
        jnp.bfloat16
    )
    return (layer_out, weight_grad, query_grad, key_grad, value_grad)


def solution(mesh):
    return jax.shard_map(
        per_device,
        mesh=mesh,
        in_specs=(
            P("dp", None, "psg"),
            P("dp", "psg", None, None),
            P("dp", "psg", None, None),
            P("dp", "psg"),
            P("psg", None),
            P("dp", None, "psg"),
        ),
        out_specs=(
            P("dp", None, "psg"),
            P("psg", None),
            P("dp", None, "psg"),
            P("dp", "psg", None, None),
            P("dp", "psg", None, None),
        ),
        check_vma=False,
    )
```

profile of v0, /device:TPU:0, one launch (start us, length us, event | category | flops | bytes accessed | tf_op | source)
XLA Modules:
  0.0 291.0 jit_solution(12191987388623553962)
XLA Ops:
  7.2 16.8 %all_gather.3 = bf16[1,128,2048]{2,1,0:T(8,128)(2,1)S(1)} all-gather(bf16[1,128,256]{2,1,0:T(8,128)(2,1)} %param.6), channel_id=1, replica_groups=mesh['dp'=4,'psg'=8] {'psg'}, dimensions={2}, use_global_device_ids=true | all-gather | bytes 589824 | tf_op jit(solution)/shard_map/all_gather | solution.py:34
  24.4 6.3 %copy.25 = bf16[1,2,256,2048]{2,1,3,0:T(2,128)(2,1)} copy(bf16[1,2,256,2048]{3,2,1,0:T(8,128)(2,1)} %param.7) | data formatting | bytes 4194304 | tf_op args[1]
  30.7 4.4 %reshape.146 = bf16[512,32,64]{0,2,1:T(8,128)(2,1)} reshape(bf16[1,2,256,2048]{2,1,3,0:T(2,128)(2,1)} %copy.25) | data formatting | bytes 4194304 | tf_op jit(solution)/shard_map/reshape.4
  35.1 6.1 %copy.26 = bf16[1,2,256,2048]{2,1,3,0:T(2,128)(2,1)} copy(bf16[1,2,256,2048]{3,2,1,0:T(8,128)(2,1)} %param.8) | data formatting | bytes 4194304 | tf_op args[2]
  41.2 4.4 %reshape.147 = bf16[512,32,64]{0,2,1:T(8,128)(2,1)} reshape(bf16[1,2,256,2048]{2,1,3,0:T(2,128)(2,1)} %copy.26) | data formatting | bytes 4194304 | tf_op jit(solution)/shard_map/reshape.10
  45.7 6.1 %select_reduce_fusion = (f32[32,128]{1,0:T(8,128)S(1)}, f32[32,128,512]{2,1,0:T(8,128)}) fusion(pred[512]{0:T(512)(128)(4,1)S(1)} %lt.27, bf16[128,32,64]{0,2,1:T(8,128)(2,1)S(1)} %bitcast.89, bf16[512,32,64]{0,2,1:T(8,128)(2,1)} %reshape.146), kind=kOutput, calls=%fused_computation.2 | convolution fusion | flops 272625664 | bytes 11026944 | tf_op jit(solution)/shard_map/bihe,bkhe->bhik/dot_general | solution.py:42
  51.8 29.1 %pmax.7 = f32[32,128]{1,0:T(8,128)S(1)} all-reduce(f32[32,128]{1,0:T(8,128)S(1)} %get-tuple-element.19), channel_id=1, replica_groups=mesh['dp'=4,'psg'=8] {'psg'}, use_global_device_ids=true, to_apply=%region_1.2 | all-reduce | flops 4096 | bytes 32768 | tf_op jit(solution)/shard_map/pmax | solution.py:46
  81.0 5.7 %fusion.3 = f32[32,128,64]{1,2,0:T(8,128)S(1)} fusion(bf16[512,32,64]{0,2,1:T(8,128)(2,1)} %reshape.147, f32[32,128,512]{2,1,0:T(8,128)} %get-tuple-element.20, f32[32,128]{1,0:T(8,128)S(1)} %pmax.7, pred[512]{0:T(512)(128)(4,1)S(1)} %lt.27), kind=kOutput, calls=%fused_computation.6 | convolution fusion | flops 274726912 | bytes 11551232 | tf_op jit(solution)/shard_map/bhik,bkhe->bihe/dot_general | solution.py:19
  86.7 1.4 copy.27
  88.2 0.4 fusion.17
  88.6 4.6 %fusion.1 = f32[32,128]{1,0:T(8,128)S(1)} fusion(f32[32,128,512]{2,1,0:T(8,128)} %get-tuple-element.20, f32[32,128]{1,0:T(8,128)S(1)} %pmax.7, pred[512]{0:T(512)(128)(4,1)S(1)} %lt.27), kind=kLoop, calls=%fused_computation.4 | loop fusion | flops 6287360 | bytes 8421888 | tf_op jit(solution)/shard_map/reduce_sum | solution.py:49
  93.3 61.3 %all-reduce.8 = (f32[1,32,128]{2,1,0:T(8,128)S(1)}, bf16[128,2048]{1,0:T(8,128)(2,1)}) all-reduce(f32[1,32,128]{2,1,0:T(8,128)S(1)} %bitcast.95, f32[128,2048]{1,0:T(8,128)S(1)} %fusion.17), channel_id=1, replica_groups=mesh['dp'=4,'psg'=8] {'psg'}, use_global_device_ids=true, to_apply=%region_4.5 | all-reduce | flops 266240 | bytes 1605632 | tf_op jit(solution)/shard_map/psum | solution.py:48
  154.5 2.1 copy.30
  156.7 1.3 copy.28
  158.0 3.1 %convert_multiply_fusion = (f32[128,2048]{1,0:T(8,128)}, bf16[128,2048]{1,0:T(8,128)(2,1)}) fusion(bf16[128,2048]{1,0:T(8,128)(2,1)} %get-tuple-element.16, f32[128,2048]{1,0:T(8,128)} %copy.28, f32[1,128,2048]{2,1,0:T(8,128)} %all-reduce.5.cloned.1.call-done), kind=kLoop, calls=%fused_computation.21 | loop fusion | flops 1310720 | bytes 4194304 | tf_op jit(solution)/shard_map/mul | solution.py:70
  161.0 2.6 copy.31
  163.7 1.3 bitcast_reduce_fusion
  165.0 5.9 %multiply_convert_fusion = bf16[32,128,512]{2,1,0:T(8,128)(2,1)S(1)} fusion(f32[32,128]{1,0:T(8,128)S(1)} %bitcast.99, bf16[128,32,64]{0,2,1:T(8,128)(2,1)} %bitcast.93, bf16[512,32,64]{0,2,1:T(8,128)(2,1)} %reshape.147, f32[32,128]{1,0:T(8,128)S(1)} %bitcast.97, f32[32,128,512]{2,1,0:T(8,128)} %get-tuple-element.20, f32[32,128]{1,0:T(8,128)S(1)} %pmax.7, ...), kind=kOutput, calls=%fused_computation | convolution fusion | flops 281018368 | bytes 15254016 | tf_op jit(solution)/shard_map/bihe,bkhe->bhik/dot_general | solution.py:75
  170.9 2.5 fusion.23
  173.4 2.6 copy.32
  176.3 1.3 copy.29
  177.6 3.7 %fusion.10 = bf16[512,2048]{0,1:T(8,128)(2,1)} fusion(f32[1,128,2048]{2,1,0:T(8,128)} %all-reduce.5.cloned.1.call-done, f32[1,128,2048]{2,1,0:T(8,128)} %copy.29, bf16[1,128,512]{2,1,0:T(8,128)(2,1)S(1)} %copy-done.7), kind=kOutput, calls=%fused_computation.13 | convolution fusion | flops 270008320 | bytes 4325376 | tf_op jit(solution)/shard_map/dot_general | solution.py:63
  181.4 5.8 %convert_bitcast_fusion = bf16[1,512,32,64]{1,3,2,0:T(8,128)(2,1)} fusion(bf16[128,32,64]{0,2,1:T(8,128)(2,1)S(1)} %bitcast.94, f32[32,128]{1,0:T(8,128)S(1)} %bitcast.98, f32[32,128,512]{2,1,0:T(8,128)} %get-tuple-element.20, f32[32,128]{1,0:T(8,128)S(1)} %pmax.7, pred[512]{0:T(512)(128)(4,1)S(1)} %lt.27), kind=kOutput, calls=%fused_computation.14 | convolution fusion | flops 277872640 | bytes 11043328 | tf_op jit(solution)/shard_map/bhik,bihe->bkhe/dot_general | solution.py:79
  187.1 4.0 %reshape.156 = bf16[1,2,256,2048]{2,1,3,0:T(2,128)(2,1)} reshape(bf16[1,512,32,64]{1,3,2,0:T(8,128)(2,1)} %convert_bitcast_fusion) | data formatting | bytes 4194304 | tf_op jit(solution)/shard_map/reshape | solution.py:85
  191.2 6.1 %copy.35 = bf16[1,2,256,2048]{3,2,1,0:T(8,128)(2,1)} copy(bf16[1,2,256,2048]{2,1,3,0:T(2,128)(2,1)} %reshape.156) | data formatting | bytes 4194304
  197.3 4.2 %convert_bitcast_fusion.1 = bf16[1,512,32,64]{1,3,2,0:T(8,128)(2,1)} fusion(bf16[128,32,64]{0,2,1:T(8,128)(2,1)S(1)} %bitcast.90, bf16[32,128,512]{2,1,0:T(8,128)(2,1)} %copy-done.2), kind=kOutput, calls=%fused_computation.15 | convolution fusion | flops 269484032 | bytes 6815744 | tf_op jit(solution)/shard_map/bhik,bihe->bkhe/dot_general | solution.py:86
  201.6 4.0 %reshape.155 = bf16[1,2,256,2048]{2,1,3,0:T(2,128)(2,1)} reshape(bf16[1,512,32,64]{1,3,2,0:T(8,128)(2,1)} %convert_bitcast_fusion.1) | data formatting | bytes 4194304 | tf_op jit(solution)/shard_map/reshape | solution.py:89
  205.6 6.1 %copy.34 = bf16[1,2,256,2048]{3,2,1,0:T(8,128)(2,1)} copy(bf16[1,2,256,2048]{2,1,3,0:T(2,128)(2,1)} %reshape.155) | data formatting | bytes 4194304
  211.7 1.5 fusion.14
  213.2 1.5 convert_element_type.83
  214.8 65.7 %all-reduce.7.cloned.1.call-done = bf16[512,2048]{0,1:T(8,128)(2,1)} async-done(((bf16[512,2048]{0,1:T(8,128)(2,1)}), bf16[512,2048]{0,1:T(8,128)(2,1)}) %all-reduce.7.cloned.1.call-update) | async-done | bytes 2097168 | tf_op jit(solution)/shard_map/psum | solution.py:62
  280.4 4.1 %copy.33 = f32[512,2048]{1,0:T(8,128)} copy(bf16[512,2048]{0,1:T(8,128)(2,1)} %all-reduce.7.cloned.1.call-done) | data formatting | bytes 6291456
  (32 shorter events, 0.8 us)
Async XLA Ops:
  7.2 81.0 %copy-start = (bf16[512,2048]{1,0:T(8,128)(2,1)S(1)}, bf16[512,2048]{1,0:T(8,128)(2,1)}, u32[]{:S(2)}) copy-start(bf16[512,2048]{1,0:T(8,128)(2,1)} %param.10) | copy-start | bytes 6291460
  7.2 150.8 %all-reduce.5.cloned.1.call-start = ((), (), s32[]{:S(2)}) async-start(), calls=%async_computation.1 | async-start | bytes 2097152 | tf_op jit(solution)/shard_map/psum | solution.py:48
  24.4 21.3 %copy-start.3 = (bf16[1,128,2048]{1,2,0:T(8,128)(2,1)}, bf16[1,128,2048]{1,2,0:T(8,128)(2,1)S(1)}, u32[]{:S(2)}) copy-start(bf16[1,128,2048]{1,2,0:T(8,128)(2,1)S(1)} %copy.24) | copy-start | bytes 1572868
  35.1 10.5 %copy-start.8 = (s32[1,2]{1,0:T(1,128)S(1)}, s32[1,2]{1,0:T(1,128)}, u32[]{:S(2)}) copy-start(s32[1,2]{1,0:T(1,128)} %param.9) | copy-start | bytes 28
  80.9 7.2 %copy-start.7 = (bf16[1,128,512]{2,1,0:T(8,128)(2,1)S(1)}, bf16[1,128,512]{2,1,0:T(8,128)(2,1)}, u32[]{:S(2)}) copy-start(bf16[1,128,512]{2,1,0:T(8,128)(2,1)} %param.11) | copy-start | bytes 393220
  88.1 125.1 %reduce-scatter.2.cloned.1.call-start = ((), (), s32[]{:S(2)}) async-start(), calls=%async_computation.3 | async-start | bytes 1179648 | tf_op jit(solution)/shard_map/reduce_scatter | solution.py:94
  165.0 5.9 %copy-start.1 = (bf16[512,32,64]{0,2,1:T(8,128)(2,1)S(1)}, bf16[512,32,64]{0,2,1:T(8,128)(2,1)}, u32[]{:S(2)}) copy-start(bf16[512,32,64]{0,2,1:T(8,128)(2,1)} %reshape.146) | copy-start | bytes 6291460
  170.9 2.5 copy-start.2
  176.1 104.4 %all-reduce.7.cloned.1.call-start = ((), (), s32[]{:S(2)}) async-start(), calls=%async_computation.2 | async-start | bytes 4194304 | tf_op jit(solution)/shard_map/psum | solution.py:62
  177.6 3.8 %copy-start.6 = (bf16[128,2048]{0,1:T(8,128)(2,1)S(1)}, bf16[128,2048]{0,1:T(8,128)(2,1)}, u32[]{:S(2)}) copy-start(bf16[128,2048]{0,1:T(8,128)(2,1)} %copy.30) | copy-start | bytes 1572868
  187.1 10.2 %copy-start.4 = (bf16[1,128,2048]{1,2,0:T(8,128)(2,1)S(1)}, bf16[1,128,2048]{1,2,0:T(8,128)(2,1)}, u32[]{:S(2)}) copy-start(bf16[1,128,2048]{1,2,0:T(8,128)(2,1)} %copy-done.3) | copy-start | bytes 1572868
  201.6 10.2 %copy-start.5 = (bf16[128,2048]{1,0:T(8,128)(2,1)S(1)}, bf16[128,2048]{1,0:T(8,128)(2,1)}, u32[]{:S(2)}) copy-start(bf16[128,2048]{1,0:T(8,128)(2,1)} %get-tuple-element.18) | copy-start | bytes 1572868
Sparse Core Ops, SparseCore 0:
  88.2 63.2 all-reduce.4
  176.2 33.2 reduce-scatter.1
  212.6 67.7 all-reduce.6
where the time goes:
time: 292 us; the launch traced here: 291 us
  blocking collectives  107 us (37%)
  waiting for transfers between devices  65.7 us (22%)
  local copies, waits for them, and re-layouts  57.4 us (20%)
  matrix products  35.9 us (12%)
  between operations  13.9 us (5%)
  other arithmetic  10.6 us (4%)
    psum x1, waiting for transfers between devices, per_device(): lax.psum(jnp.dot(grad_rows.T, context_rows, preferred_element_type=jnp.fl...  65.7 us
    psum x1, blocking collectives, per_device(): lax.psum((jnp.sum(weights, axis=3), weighted_values(weights, value_heads)...  61.3 us
    pmax x1, blocking collectives, per_device(): row_max = lax.pmax(local_max, 'psg')  29.1 us
    unnamed x25, local copies, waits for them, and re-layouts  28.9 us
    all_gather x1, blocking collectives, per_device(): query_full = lax.all_gather(queries, 'psg', axis=2, tiled=True)  16.8 us
    another operation x2, local copies, waits for them, and re-layouts  8.74 us
    dot_general x1, matrix products, per_device(): jnp.einsum('bihe,bkhe->bhik', query_heads, key_heads, preferred_element_t...  6.12 us
    dot_general x1, matrix products, per_device(): jnp.einsum('bihe,bkhe->bhik', grad_heads, value_heads, preferred_element_...  5.91 us
  transfers between devices with their start and end apart: 3, of which 1 were waited for; matrix products, arithmetic and copies ran while one was open for 16% of the time, Pallas kernels for 0%

commit v1 on v0

--- a/solution.py
+++ b/solution.py
@@ -59,9 +59,14 @@
         jnp.bfloat16
     )
     layer_out = layer_out.reshape(question_count, answer_len, -1)
-    weight_grad = lax.psum(
-        jnp.dot(grad_rows.T, context_rows, preferred_element_type=jnp.float32).astype(jnp.bfloat16),
-        "dp",
+    weight_grad = jnp.sum(
+        lax.all_gather(
+            jnp.dot(grad_rows.T, context_rows, preferred_element_type=jnp.float32).astype(
+                jnp.bfloat16
+            ),
+            "dp",
+        ),
+        0,
     ).astype(jnp.float32)
     context_grad = lax.psum(
         jnp.dot(grad_rows, out_weight, preferred_element_type=jnp.float32), "psg"

time: 292 us -> 338 us (1.16)
  waiting for transfers between devices: 65.7 us -> 82.6 us
  other arithmetic: 10.6 us -> 25.6 us
  local copies, waits for them, and re-layouts: 57.4 us -> 71.6 us
    all_gather x0 -> x1, waiting for transfers between devices: none -> 82.6 us  [per_device(): lax.all_gather(jnp.dot(grad_rows.T, context_rows, preferred_element_type=...]
    psum x1 -> x0, waiting for transfers between devices: 65.7 us -> none  [per_device(): lax.psum(jnp.dot(grad_rows.T, context_rows, preferred_element_type=jnp.fl...]
    reduce_sum x0 -> x1, other arithmetic: none -> 15 us  [per_device(): jnp.sum(lax.all_gather(jnp.dot(grad_rows.T, context_rows, preferred_eleme...]
    all_gather x0 -> x1, local copies, waits for them, and re-layouts: none -> 14.5 us  [per_device(): lax.all_gather(jnp.dot(grad_rows.T, context_rows, preferred_element_type=...]
    unnamed x25 -> x27, local copies, waits for them, and re-layouts: 28.9 us -> 28.8 us
  transfers between devices with their start and end apart: 3 -> 3, of which waited for: 1 -> 1; matrix products, arithmetic and copies ran while one was open for 16% -> 14% of each run, Pallas kernels for 0% -> 0%
where the time goes in v1:
time: 338 us; the launch traced here: 336 us
  blocking collectives  106 us (31%)
  waiting for transfers between devices  82.6 us (24%)
  local copies, waits for them, and re-layouts  71.6 us (21%)
  matrix products  36 us (11%)
  other arithmetic  25.6 us (8%)
  between operations  13.9 us (4%)
    all_gather x1, waiting for transfers between devices, per_device(): lax.all_gather(jnp.dot(grad_rows.T, context_rows, preferred_element_type=...  82.6 us
    psum x1, blocking collectives, per_device(): lax.psum((jnp.sum(weights, axis=3), weighted_values(weights, value_heads)...  60.4 us
    pmax x1, blocking collectives, per_device(): row_max = lax.pmax(local_max, 'psg')  29.1 us
    unnamed x27, local copies, waits for them, and re-layouts  28.8 us
    all_gather x1, blocking collectives, per_device(): query_full = lax.all_gather(queries, 'psg', axis=2, tiled=True)  16.5 us
    reduce_sum x1, other arithmetic, per_device(): jnp.sum(lax.all_gather(jnp.dot(grad_rows.T, context_rows, preferred_eleme...  15 us
    all_gather x1, local copies, waits for them, and re-layouts, per_device(): lax.all_gather(jnp.dot(grad_rows.T, context_rows, preferred_element_type=...  14.5 us
    another operation x2, local copies, waits for them, and re-layouts  8.74 us
  transfers between devices with their start and end apart: 3, of which 1 were waited for; matrix products, arithmetic and copies ran while one was open for 14% of the time, Pallas kernels for 0%

profile of v1, /device:TPU:0, one launch (start us, length us, event | category | flops | bytes accessed | tf_op | source)
XLA Modules:
  0.0 336.0 jit_solution(1150715187759157749)
XLA Ops:
  7.3 6.3 %copy.35 = bf16[1,2,256,2048]{2,1,3,0:T(2,128)(2,1)} copy(bf16[1,2,256,2048]{3,2,1,0:T(8,128)(2,1)} %param.7) | data formatting | bytes 4194304 | tf_op args[1]
  13.5 4.4 %reshape.146 = bf16[512,32,64]{0,2,1:T(8,128)(2,1)} reshape(bf16[1,2,256,2048]{2,1,3,0:T(2,128)(2,1)} %copy.35) | data formatting | bytes 4194304 | tf_op jit(solution)/shard_map/reshape.4
  17.9 16.5 %all_gather.9 = bf16[1,128,2048]{2,1,0:T(8,128)(2,1)S(1)} all-gather(bf16[1,128,256]{2,1,0:T(8,128)(2,1)S(1)} %copy-done.8), channel_id=1, replica_groups=mesh['dp'=4,'psg'=8] {'psg'}, dimensions={2}, use_global_device_ids=true | all-gather | bytes 589824 | tf_op jit(solution)/shard_map/all_gather | solution.py:34
  34.8 6.2 %select_reduce_fusion = (f32[32,128]{1,0:T(8,128)S(1)}, f32[32,128,512]{2,1,0:T(8,128)}) fusion(pred[512]{0:T(512)(128)(4,1)S(1)} %lt.27, bf16[128,32,64]{0,2,1:T(8,128)(2,1)S(1)} %bitcast.91, bf16[512,32,64]{0,2,1:T(8,128)(2,1)} %reshape.146), kind=kOutput, calls=%fused_computation.2 | convolution fusion | flops 272625664 | bytes 11026944 | tf_op jit(solution)/shard_map/bihe,bkhe->bhik/dot_general | solution.py:42
  41.0 29.1 %pmax.7 = f32[32,128]{1,0:T(8,128)S(1)} all-reduce(f32[32,128]{1,0:T(8,128)S(1)} %get-tuple-element.24), channel_id=1, replica_groups=mesh['dp'=4,'psg'=8] {'psg'}, use_global_device_ids=true, to_apply=%region_1.2 | all-reduce | flops 4096 | bytes 32768 | tf_op jit(solution)/shard_map/pmax | solution.py:46
  70.2 6.1 %copy.36 = bf16[1,2,256,2048]{2,1,3,0:T(2,128)(2,1)} copy(bf16[1,2,256,2048]{3,2,1,0:T(8,128)(2,1)} %param.8) | data formatting | bytes 4194304 | tf_op args[2]
  76.3 4.4 %reshape.147 = bf16[512,32,64]{0,2,1:T(8,128)(2,1)} reshape(bf16[1,2,256,2048]{2,1,3,0:T(2,128)(2,1)} %copy.36) | data formatting | bytes 4194304 | tf_op jit(solution)/shard_map/reshape.10
  80.7 5.7 %fusion.3 = f32[32,128,64]{1,2,0:T(8,128)S(1)} fusion(bf16[512,32,64]{0,2,1:T(8,128)(2,1)} %reshape.147, f32[32,128,512]{2,1,0:T(8,128)} %get-tuple-element.25, f32[32,128]{1,0:T(8,128)S(1)} %pmax.7, pred[512]{0:T(512)(128)(4,1)S(1)} %lt.27), kind=kOutput, calls=%fused_computation.6 | convolution fusion | flops 274726912 | bytes 11551232 | tf_op jit(solution)/shard_map/bhik,bkhe->bihe/dot_general | solution.py:19
  86.4 1.3 copy.37
  88.2 4.6 %fusion.1 = f32[32,128]{1,0:T(8,128)S(1)} fusion(f32[32,128,512]{2,1,0:T(8,128)} %get-tuple-element.25, f32[32,128]{1,0:T(8,128)S(1)} %pmax.7, pred[512]{0:T(512)(128)(4,1)S(1)} %lt.27), kind=kLoop, calls=%fused_computation.4 | loop fusion | flops 6287360 | bytes 8421888 | tf_op jit(solution)/shard_map/reduce_sum | solution.py:49
  92.9 60.4 %all-reduce.5 = (f32[1,32,128]{2,1,0:T(8,128)S(1)}, bf16[128,2048]{1,0:T(8,128)(2,1)}) all-reduce(f32[1,32,128]{2,1,0:T(8,128)S(1)} %bitcast.97, f32[128,2048]{1,0:T(8,128)S(1)} %fusion.17), channel_id=1, replica_groups=mesh['dp'=4,'psg'=8] {'psg'}, use_global_device_ids=true, to_apply=%region_4.5 | all-reduce | flops 266240 | bytes 1605632 | tf_op jit(solution)/shard_map/psum | solution.py:48
  153.3 2.0 copy.40
  155.4 1.3 copy.38
  156.7 3.1 convert_multiply_fusion
  159.8 2.5 copy.41
  162.3 1.3 bitcast_reduce_fusion
  163.7 5.9 %multiply_convert_fusion = bf16[32,128,512]{2,1,0:T(8,128)(2,1)S(1)} fusion(f32[32,128]{1,0:T(8,128)S(1)} %bitcast.101, bf16[128,32,64]{0,2,1:T(8,128)(2,1)} %bitcast.95, bf16[512,32,64]{0,2,1:T(8,128)(2,1)} %reshape.147, f32[32,128]{1,0:T(8,128)S(1)} %bitcast.99, f32[32,128,512]{2,1,0:T(8,128)} %get-tuple-element.25, f32[32,128]{1,0:T(8,128)S(1)} %pmax.7, ...), kind=kOutput, calls=%fused_computation | convolution fusion | flops 281018368 | bytes 15254016 | tf_op jit(solution)/shard_map/bihe,bkhe->bhik/dot_general | solution.py:80
  169.6 2.5 fusion.23
  172.1 2.5 copy.42
  176.2 3.7 %fusion.10 = bf16[512,2048]{0,1:T(8,128)(2,1)} fusion(f32[1,128,2048]{2,1,0:T(8,128)} %all-reduce.4.cloned.1.call-done, f32[1,128,2048]{2,1,0:T(8,128)} %copy.39, bf16[1,128,512]{2,1,0:T(8,128)(2,1)S(1)} %copy-done.7), kind=kOutput, calls=%fused_computation.13 | convolution fusion | flops 270008320 | bytes 4325376 | tf_op jit(solution)/shard_map/dot_general | solution.py:64
  179.9 5.8 %convert_bitcast_fusion = bf16[1,512,32,64]{1,3,2,0:T(8,128)(2,1)} fusion(bf16[128,32,64]{0,2,1:T(8,128)(2,1)S(1)} %bitcast.96, f32[32,128]{1,0:T(8,128)S(1)} %bitcast.100, f32[32,128,512]{2,1,0:T(8,128)} %get-tuple-element.25, f32[32,128]{1,0:T(8,128)S(1)} %pmax.7, pred[512]{0:T(512)(128)(4,1)S(1)} %lt.27), kind=kOutput, calls=%fused_computation.14 | convolution fusion | flops 277872640 | bytes 11043328 | tf_op jit(solution)/shard_map/bhik,bihe->bkhe/dot_general | solution.py:84
  185.7 4.0 %reshape.156 = bf16[1,2,256,2048]{2,1,3,0:T(2,128)(2,1)} reshape(bf16[1,512,32,64]{1,3,2,0:T(8,128)(2,1)} %convert_bitcast_fusion) | data formatting | bytes 4194304 | tf_op jit(solution)/shard_map/reshape | solution.py:90
  189.7 6.1 %copy.45 = bf16[1,2,256,2048]{3,2,1,0:T(8,128)(2,1)} copy(bf16[1,2,256,2048]{2,1,3,0:T(2,128)(2,1)} %reshape.156) | data formatting | bytes 4194304
  195.9 4.2 %convert_bitcast_fusion.1 = bf16[1,512,32,64]{1,3,2,0:T(8,128)(2,1)} fusion(bf16[128,32,64]{0,2,1:T(8,128)(2,1)S(1)} %bitcast.92, bf16[32,128,512]{2,1,0:T(8,128)(2,1)} %copy-done.2), kind=kOutput, calls=%fused_computation.15 | convolution fusion | flops 269484032 | bytes 6815744 | tf_op jit(solution)/shard_map/bhik,bihe->bkhe/dot_general | solution.py:91
  200.1 4.0 %reshape.155 = bf16[1,2,256,2048]{2,1,3,0:T(2,128)(2,1)} reshape(bf16[1,512,32,64]{1,3,2,0:T(8,128)(2,1)} %convert_bitcast_fusion.1) | data formatting | bytes 4194304 | tf_op jit(solution)/shard_map/reshape | solution.py:94
  204.2 6.1 %copy.44 = bf16[1,2,256,2048]{3,2,1,0:T(8,128)(2,1)} copy(bf16[1,2,256,2048]{2,1,3,0:T(2,128)(2,1)} %reshape.155) | data formatting | bytes 4194304
  210.3 1.5 fusion.14
  211.8 1.5 convert_element_type.85
  213.3 82.6 %all-gather.3.cloned.1.call-done = bf16[2048,2048]{0,1:T(8,128)(2,1)} async-done(((bf16[512,2048]{0,1:T(8,128)(2,1)}), bf16[2048,2048]{0,1:T(8,128)(2,1)}) %all-gather.3.cloned.1.call-update) | async-done | bytes 8388624 | tf_op jit(solution)/shard_map/all_gather | solution.py:63
  295.9 14.5 %reshape.158 = bf16[4,512,2048]{1,0,2:T(4,128)(2,1)} reshape(bf16[2048,2048]{0,1:T(8,128)(2,1)} %all-gather.3.cloned.1.call-done) | data formatting | bytes 16777216 | tf_op jit(solution)/shard_map/all_gather | solution.py:63
  310.4 15.0 %reduce_sum.36 = bf16[512,2048]{0,1:T(8,128)(2,1)} reduce(bf16[4,512,2048]{1,0,2:T(4,128)(2,1)} %reshape.158, bf16[]{:T(256)} %constant.5.clone.1), dimensions={0}, to_apply=%region_5.6 | reduce | flops 3145728 | bytes 10485762 | tf_op jit(solution)/shard_map/reduce_sum | solution.py:62
  325.4 4.1 %copy.43 = f32[512,2048]{1,0:T(8,128)} copy(bf16[512,2048]{0,1:T(8,128)(2,1)} %reduce_sum.36) | data formatting | bytes 6291456
  (36 shorter events, 2.6 us)
Async XLA Ops:
  7.2 80.6 %copy-start = (bf16[512,2048]{1,0:T(8,128)(2,1)S(1)}, bf16[512,2048]{1,0:T(8,128)(2,1)}, u32[]{:S(2)}) copy-start(bf16[512,2048]{1,0:T(8,128)(2,1)} %param.10) | copy-start | bytes 6291460
  7.2 149.6 %all-reduce.4.cloned.1.call-start = ((), (), s32[]{:S(2)}) async-start(), calls=%async_computation.1 | async-start | bytes 2097152 | tf_op jit(solution)/shard_map/psum | solution.py:48
  7.2 10.7 %copy-start.8 = (bf16[1,128,256]{2,1,0:T(8,128)(2,1)S(1)}, bf16[1,128,256]{2,1,0:T(8,128)(2,1)}, u32[]{:S(2)}) copy-start(bf16[1,128,256]{2,1,0:T(8,128)(2,1)} %param.6) | copy-start | bytes 196612
  7.3 27.4 %copy-start.9 = (s32[1,2]{1,0:T(1,128)S(1)}, s32[1,2]{1,0:T(1,128)}, u32[]{:S(2)}) copy-start(s32[1,2]{1,0:T(1,128)} %param.9) | copy-start | bytes 28
  34.7 6.3 %copy-start.3 = (bf16[1,128,2048]{1,2,0:T(8,128)(2,1)}, bf16[1,128,2048]{1,2,0:T(8,128)(2,1)S(1)}, u32[]{:S(2)}) copy-start(bf16[1,128,2048]{1,2,0:T(8,128)(2,1)S(1)} %copy.34) | copy-start | bytes 1572868
  80.7 7.1 %copy-start.7 = (bf16[1,128,512]{2,1,0:T(8,128)(2,1)S(1)}, bf16[1,128,512]{2,1,0:T(8,128)(2,1)}, u32[]{:S(2)}) copy-start(bf16[1,128,512]{2,1,0:T(8,128)(2,1)} %param.11) | copy-start | bytes 393220
  87.7 124.1 %reduce-scatter.2.cloned.1.call-start = ((), (), s32[]{:S(2)}) async-start(), calls=%async_computation.2 | async-start | bytes 1179648 | tf_op jit(solution)/shard_map/reduce_scatter | solution.py:99
  163.6 5.9 %copy-start.1 = (bf16[512,32,64]{0,2,1:T(8,128)(2,1)S(1)}, bf16[512,32,64]{0,2,1:T(8,128)(2,1)}, u32[]{:S(2)}) copy-start(bf16[512,32,64]{0,2,1:T(8,128)(2,1)} %reshape.146) | copy-start | bytes 6291460
  169.6 2.5 copy-start.2
  174.7 121.3 %all-gather.3.cloned.1.call-start = ((), (), s32[]{:S(2)}) async-start(), calls=%async_computation.3 | async-start | bytes 10485760 | tf_op jit(solution)/shard_map/all_gather | solution.py:63
  176.2 3.7 %copy-start.6 = (bf16[128,2048]{0,1:T(8,128)(2,1)S(1)}, bf16[128,2048]{0,1:T(8,128)(2,1)}, u32[]{:S(2)}) copy-start(bf16[128,2048]{0,1:T(8,128)(2,1)} %copy.40) | copy-start | bytes 1572868
  185.7 10.2 %copy-start.4 = (bf16[1,128,2048]{1,2,0:T(8,128)(2,1)S(1)}, bf16[1,128,2048]{1,2,0:T(8,128)(2,1)}, u32[]{:S(2)}) copy-start(bf16[1,128,2048]{1,2,0:T(8,128)(2,1)} %copy-done.3) | copy-start | bytes 1572868
  200.1 10.2 %copy-start.5 = (bf16[128,2048]{1,0:T(8,128)(2,1)S(1)}, bf16[128,2048]{1,0:T(8,128)(2,1)}, u32[]{:S(2)}) copy-start(bf16[128,2048]{1,0:T(8,128)(2,1)} %get-tuple-element.23) | copy-start | bytes 1572868
Sparse Core Ops, SparseCore 0:
  87.8 63.1 all-reduce.3
  174.8 33.7 reduce-scatter.1
  210.4 85.5 all-gather.2
